TPU v7x, 32 devices: a whole 2x2x4 slice. The times are simulated.
32 devices in a mesh: groups: 2 (over x), ctx: 16 (over z, y, core).
Axes of the slice: x: 2, y: 2, z: 4, core: 2. Of those that a mesh axis runs over, the one named last changes fastest.
Arguments:
- tokens: bfloat16 [3072, 1152], P(('groups', 'ctx')), parts along dimension 0, may hold values from -100 to 100
- owner: int32 [3072, 1], P(('groups', 'ctx')), parts along dimension 0, may hold values from 0 to 15; in each aligned block of 96 rows (0 to 95, 96 to 191, ...) at most 12 rows name the same one
- slot_map: int32 [32, 16, 12], P(('groups', 'ctx')), parts along dimension 0, may hold values from 0 to 47
- sizes: int32 [3072], P(('groups', 'ctx')), parts along dimension 0, may hold values from 1 to 4
- w_query: bfloat16 [1152, 576], replicated, may hold values from -0.1875 to 0.1875
- w_key: bfloat16 [1152, 576], replicated, may hold values from -0.1875 to 0.1875
- w_value: bfloat16 [1152, 576], replicated, may hold values from -0.1875 to 0.1875
- w_out: bfloat16 [576, 1152], replicated, may hold values from -0.25 to 0.25
Outputs:
- mixed: bfloat16 [3072, 1152], P(('groups', 'ctx')), parts along dimension 0
There are 2 independent parts, one for each index of `groups`. A program takes and returns all parts, laid end to end along the dimension named above; an argument that names none is the same for every part. Nothing has to cross between parts.
Inputs may be any that keep to these rules, and one draw needn't show every extreme that they name: Among the source tokens of one index of ctx, at most 12 name the same owner, and in some index exactly 12 do.
All inputs are finite; a program needn't handle non-finite values.
Results may differ from a plain program's by a relative error of at most 0.0085.
The roundings to bfloat16 on the way count: a program that leaves them out, or rounds other values in their place, can miss the bound.
Values may be sent and summed in bfloat16 or wider, within the bound.
A program may use at most 128 MiB of HBM per device.

v0:
```python
import math
import jax
import jax.numpy as jnp
from jax import lax
from jax.sharding import PartitionSpec as P

HEADS = 8
HEAD = 72


def on_device(tokens, owner, slot_map, sizes, w_query, w_key, w_value, w_out):
    tok_rows = tokens.shape[0]
    shards = lax.axis_size("ctx")
    slots = slot_map.shape[2]
    places = shards * slots
    merged_rows = tok_rows // 2
    owners = owner[:, 0]
    marks = (owners[:, None] == jnp.arange(shards, dtype=jnp.int32)[None, :]).astype(jnp.int32)
    ranking = jnp.sum((jnp.cumsum(marks, axis=0) - marks) * marks, axis=1)
    bucket = owners * slots + ranking
    to_bucket = (bucket[:, None] == jnp.arange(places, dtype=jnp.int32)[None, :]).astype(
        jnp.bfloat16
    )
    outgoing = jnp.einsum(
        "tp,td->pd", to_bucket, tokens, preferred_element_type=jnp.float32
    ).astype(jnp.bfloat16)
    out_weights = jnp.einsum(
        "tp,t->p", to_bucket, sizes.astype(jnp.bfloat16), preferred_element_type=jnp.float32
    ).astype(jnp.bfloat16)
    received, in_weights = (
        lax.all_to_all(
            outgoing.reshape(shards, slots, -1), "ctx", split_axis=0, concat_axis=0, tiled=True
        ),
        lax.all_to_all(
            out_weights.reshape(shards, slots), "ctx", split_axis=0, concat_axis=0, tiled=True
        ),
    )
    targets = slot_map[0].reshape(places)
    landing = targets[None, :] == jnp.arange(merged_rows, dtype=jnp.int32)[:, None]
    weighted = jnp.where(landing, in_weights.reshape(places)[None, :], 0)
    merged_sum = jnp.dot(weighted, received.reshape(places, -1), preferred_element_type=jnp.float32)
    counts = jnp.sum(weighted.astype(jnp.float32), axis=1)
    merged = (merged_sum / jnp.maximum(counts, 1.0)[:, None]).astype(jnp.bfloat16)
    key_bias = jnp.where(counts > 0, jnp.log(jnp.maximum(counts, 1.0)), -1e30).astype(jnp.bfloat16)
    queries = jnp.dot(merged, w_query, preferred_element_type=jnp.float32).astype(jnp.bfloat16)
    query_heads = queries.reshape(merged_rows, HEADS, HEAD)
    inverse = 1.0 / math.sqrt(HEAD)

    def attend_block(carry, item):
        row_max, total, accum = carry
        key_heads, value_heads, bias = item
        scores = (
            jnp.einsum("qhd,khd->hqk", query_heads, key_heads, preferred_element_type=jnp.float32)
            * inverse
        )
        scores = scores + bias.astype(jnp.float32)[None, None, :]
        new_max = jnp.maximum(row_max, jnp.max(scores, axis=2))
        factor = jnp.exp(row_max - new_max)
        expo = jnp.exp(scores - new_max[:, :, None])
        total = total * factor + jnp.sum(expo, axis=2)
        accum = accum * factor[:, :, None] + jnp.einsum(
            "hqk,khd->hqd",
            expo.astype(jnp.bfloat16),
            value_heads,
            preferred_element_type=jnp.float32,
        )
        return ((new_max, total, accum), None)

    start_state = (
        jnp.full((HEADS, merged_rows), -jnp.inf, jnp.float32),
        jnp.zeros((HEADS, merged_rows), jnp.float32),
        jnp.zeros((HEADS, merged_rows, HEAD), jnp.float32),
    )
    own_keys = jnp.dot(merged, w_key, preferred_element_type=jnp.float32).astype(jnp.bfloat16)
    own_values = jnp.dot(merged, w_value, preferred_element_type=jnp.float32).astype(jnp.bfloat16)
    carry = start_state
    keys = lax.all_gather(own_keys, "ctx", axis=0, tiled=True)
    values = lax.all_gather(own_values, "ctx", axis=0, tiled=True)
    bias = lax.all_gather(key_bias, "ctx", axis=0, tiled=True)
    length = keys.shape[0]
    block = math.gcd(length, 1536)
    turns = length // block
    items = (
        keys.reshape(turns, block, HEADS, HEAD),
        values.reshape(turns, block, HEADS, HEAD),
        bias.reshape(turns, block),
    )
    carry, unused = lax.scan(attend_block, carry, items)
    row_max, total, accum = carry
    attended = (
        jnp.transpose(accum / total[:, :, None], (1, 0, 2))
        .reshape(merged_rows, HEADS * HEAD)
        .astype(jnp.bfloat16)
    )
    landing_rows = landing.astype(jnp.bfloat16)
    leaving = jnp.einsum(
        "mp,md->pd", landing_rows, attended, preferred_element_type=jnp.float32
    ).astype(jnp.bfloat16)
    returned = lax.all_to_all(
        leaving.reshape(shards, slots, -1), "ctx", split_axis=0, concat_axis=0, tiled=True
    )
    picked = jnp.einsum(
        "tp,pd->td", to_bucket, returned.reshape(places, -1), preferred_element_type=jnp.float32
    ).astype(jnp.bfloat16)
    mixed = jnp.dot(picked, w_out, preferred_element_type=jnp.float32).astype(jnp.bfloat16)
    return mixed


def solution(mesh):
    in_specs = (
        P(("groups", "ctx"), None),
        P(("groups", "ctx"), None),
        P(("groups", "ctx"), None, None),
        P(("groups", "ctx")),
        P(),
        P(),
        P(),
        P(),
    )
    out_specs = P(("groups", "ctx"), None)
    return jax.shard_map(
        on_device, mesh=mesh, in_specs=in_specs, out_specs=out_specs, check_vma=False
    )
```

profile of v0, /device:TPU:0, one launch (start us, length us, event | category | flops | bytes accessed | tf_op | source)
XLA Modules:
  0.0 126.5 jit_solution(1130961317788527914)
XLA Ops:
  0.0 0.0 copy-start
  0.0 0.8 fusion.16
  0.8 0.1 reduce_window_sum.11
  1.0 0.8 select_reduce_fusion
  1.8 0.7 fusion.23
  2.5 0.8 fusion.10
  3.3 0.7 all_to_all.16
  4.1 7.4 %all-to-all-start = ((bf16[16,1,12]{2,1,0:T(2,128)(2,1)}), bf16[16,1,12]{2,1,0:T(2,128)(2,1)S(1)}, u32[]{:S(2)}, u32[]{:S(2)}) async-start(bf16[16,1,12]{2,1,0:T(2,128)(2,1)} %all_to_all.16), calls=%async_computation | async-start | bytes 16384 | tf_op jit(solution)/shard_map/all_to_all | solution.py:34
  11.5 0.0 copy-start.3
  11.5 0.0 copy-start.4
  11.5 1.3 %convolution_convert_fusion = bf16[192,1152]{1,0:T(8,128)(2,1)S(1)} fusion(bf16[96,1152]{1,0:T(8,128)(2,1)} %param.8, s32[96]{0:T(128)S(1)} %fusion.23), kind=kOutput, calls=%fused_computation | convolution fusion | flops 42706944 | bytes 663936 | tf_op jit(solution)/shard_map/tp,td->pd/dot_general | solution.py:24
  12.8 0.9 reshape.49
  13.8 4.1 %all-to-all-done = bf16[16,1,12]{2,1,0:T(2,128)(2,1)S(1)} async-done(((bf16[16,1,12]{2,1,0:T(2,128)(2,1)}), bf16[16,1,12]{2,1,0:T(2,128)(2,1)S(1)}, u32[]{:S(2)}, u32[]{:S(2)}) %all-to-all-start) | async-done | bytes 416 | tf_op jit(solution)/shard_map/all_to_all | solution.py:34
  17.8 3.6 %all-to-all-start.1 = ((bf16[16,12,1152]{2,1,0:T(8,128)(2,1)}), bf16[16,12,1152]{2,1,0:T(8,128)(2,1)S(1)}, u32[]{:S(2)}, u32[]{:S(2)}) async-start(bf16[16,12,1152]{2,1,0:T(8,128)(2,1)} %reshape.49), calls=%async_computation.1 | async-start | bytes 1179648 | tf_op jit(solution)/shard_map/all_to_all | solution.py:31
  21.4 0.0 copy-start.1
  21.4 0.0 copy-done.3
  21.5 0.1 copy.23
  21.5 0.1 eq.53
  21.6 0.0 copy-done.4
  21.6 0.6 dynamic-slice.1
  22.9 0.1 broadcast_in_dim.39
  23.0 0.1 convert_reduce_fusion
  23.2 0.2 dynamic-update-slice
  23.4 35.8 %all-reduce = bf16[768]{0:T(1024)(128)(2,1)S(1)} all-reduce(bf16[768]{0:T(1024)(128)(2,1)S(1)} %dynamic-update-slice), channel_id=1, replica_groups=mesh['groups'=2,'ctx'=16] {'ctx'}, use_global_device_ids=true, to_apply=%add | all-reduce | flops 768 | bytes 3072
  59.2 0.0 all-to-all-done.1
  59.2 0.9 reshape.50
  60.1 1.2 fusion
  61.3 0.0 copy-done.1
  61.3 0.5 convolution_convert_fusion.4
  61.8 20.4 %all_gather.11 = bf16[768,576]{1,0:T(8,128)(2,1)S(1)} all-gather(bf16[48,576]{1,0:T(8,128)(2,1)S(1)} %convolution_convert_fusion.4), channel_id=1, replica_groups=mesh['groups'=2,'ctx'=16] {'ctx'}, dimensions={0}, use_global_device_ids=true | all-gather | bytes 940032 | tf_op jit(solution)/shard_map/all_gather | solution.py:78
  82.2 1.3 %copy.27 = bf16[768,576]{0,1:T(8,128)(2,1)} copy(bf16[768,576]{1,0:T(8,128)(2,1)S(1)} %all_gather.11) | data formatting | bytes 1769472 | tf_op jit(solution)/shard_map/all_gather | solution.py:78
  83.4 1.8 %convolution_convert_fusion.5 = bf16[48,576]{1,0:T(8,128)(2,1)S(1)} fusion(bf16[48,1152]{1,0:T(8,128)(2,1)S(1)} %fusion, bf16[1152,576]{0,1:T(8,128)(2,1)} %param.13), kind=kOutput, calls=%fused_computation.14 | convolution fusion | flops 63728640 | bytes 1492992 | tf_op jit(solution)/shard_map/dot_general | solution.py:74
  85.2 21.5 %all_gather.9 = bf16[768,576]{1,0:T(8,128)(2,1)S(1)} all-gather(bf16[48,576]{1,0:T(8,128)(2,1)S(1)} %convolution_convert_fusion.5), channel_id=1, replica_groups=mesh['groups'=2,'ctx'=16] {'ctx'}, dimensions={0}, use_global_device_ids=true | all-gather | bytes 940032 | tf_op jit(solution)/shard_map/all_gather | solution.py:77
  106.8 0.6 copy.25
  107.4 1.8 %convolution_convert_fusion.6 = bf16[48,576]{1,0:T(8,128)(2,1)S(1)} fusion(bf16[48,1152]{1,0:T(8,128)(2,1)S(1)} %fusion, bf16[1152,576]{0,1:T(8,128)(2,1)} %param.12), kind=kOutput, calls=%fused_computation.15 | convolution fusion | flops 63728640 | bytes 1492992 | tf_op jit(solution)/shard_map/dot_general | solution.py:45
  109.2 0.1 reshape.51
  109.3 0.0 copy-start.2
  109.3 0.4 fusion.25
  109.7 0.4 fusion.5
  110.1 0.4 copy-done.2
  110.5 0.4 fusion.4
  111.0 0.1 convert_element_type.72
  111.1 0.3 convolution_convert_fusion.2
  111.4 0.1 reshape.52
  111.4 13.7 %all_to_all.20 = bf16[16,12,576]{2,1,0:T(8,128)(2,1)S(1)} all-to-all(bf16[16,12,576]{2,1,0:T(8,128)(2,1)S(1)} %reshape.52), channel_id=1, replica_groups=mesh['groups'=2,'ctx'=16] {'ctx'}, dimensions={0} | all-to-all | bytes 442368 | tf_op jit(solution)/shard_map/all_to_all | solution.py:99
  125.1 0.1 reshape.53
  125.2 0.0 copy-done
  125.2 1.2 convolution_convert_fusion.1
  (8 shorter events, 0.1 us)
Async XLA Ops:
  0.0 125.2 %copy-start = (bf16[576,1152]{1,0:T(8,128)(2,1)S(1)}, bf16[576,1152]{1,0:T(8,128)(2,1)}, u32[]{:S(2)}) copy-start(bf16[576,1152]{1,0:T(8,128)(2,1)} %param.15) | copy-start | bytes 3981316
  4.1 13.8 %all-to-all-start = ((bf16[16,1,12]{2,1,0:T(2,128)(2,1)}), bf16[16,1,12]{2,1,0:T(2,128)(2,1)S(1)}, u32[]{:S(2)}, u32[]{:S(2)}) async-start(bf16[16,1,12]{2,1,0:T(2,128)(2,1)} %all_to_all.16), calls=%async_computation | async-start | bytes 16384 | tf_op jit(solution)/shard_map/all_to_all | solution.py:34
  11.5 10.0 %copy-start.3 = (s32[1,16,12]{1,0,2:T(1,128)S(1)}, s32[1,16,12]{1,0,2:T(1,128)}, u32[]{:S(2)}) copy-start(s32[1,16,12]{1,0,2:T(1,128)} %param.10) | copy-start | bytes 2308
  11.5 10.1 %copy-start.4 = (u32[32]{0:T(128)S(1)}, u32[32]{0:T(128)}, u32[]{:S(2)}) copy-start(u32[32]{0:T(128)} %constant.40) | copy-start | bytes 388
  17.8 41.4 %all-to-all-start.1 = ((bf16[16,12,1152]{2,1,0:T(8,128)(2,1)}), bf16[16,12,1152]{2,1,0:T(8,128)(2,1)S(1)}, u32[]{:S(2)}, u32[]{:S(2)}) async-start(bf16[16,12,1152]{2,1,0:T(8,128)(2,1)} %reshape.49), calls=%async_computation.1 | async-start | bytes 1179648 | tf_op jit(solution)/shard_map/all_to_all | solution.py:31
  21.4 39.9 %copy-start.1 = (bf16[1152,576]{0,1:T(8,128)(2,1)S(1)}, bf16[1152,576]{0,1:T(8,128)(2,1)}, u32[]{:S(2)}) copy-start(bf16[1152,576]{0,1:T(8,128)(2,1)} %param.14) | copy-start | bytes 3981316
  109.3 1.2 copy-start.2
where the time goes:
time: 127 us; the launch traced here: 126 us
  blocking collectives  91.4 us (72%)
  starting transfers between devices  11 us (9%)
  matrix products  9.81 us (8%)
  local copies, waits for them, and re-layouts  6.33 us (5%)
  waiting for transfers between devices  4.09 us (3%)
  other arithmetic  3.01 us (2%)
    unnamed x1, blocking collectives  35.8 us
    all_gather x1, blocking collectives, on_device(): keys = lax.all_gather(own_keys, 'ctx', axis=0, tiled=True)  21.5 us
    all_gather x1, blocking collectives, on_device(): values = lax.all_gather(own_values, 'ctx', axis=0, tiled=True)  20.4 us
    all_to_all x1, blocking collectives, on_device(): lax.all_to_all(leaving.reshape(shards, slots, -1), 'ctx', split_axis=0, c...  13.7 us
    all_to_all x1, starting transfers between devices, on_device(): lax.all_to_all(out_weights.reshape(shards, slots), 'ctx', split_axis=0, c...  7.41 us
    all_to_all x1, waiting for transfers between devices, on_device(): lax.all_to_all(out_weights.reshape(shards, slots), 'ctx', split_axis=0, c...  4.09 us
    all_to_all x1, starting transfers between devices, on_device(): lax.all_to_all(outgoing.reshape(shards, slots, -1), 'ctx', split_axis=0,...  3.58 us
  transfers between devices with their start and end apart: 2, of which 1 were waited for; matrix products, arithmetic and copies ran while one was open for 3% of the time, Pallas kernels for 0%

commit v1 on v0

--- a/solution.py
+++ b/solution.py
@@ -74,8 +74,11 @@
     own_keys = jnp.dot(merged, w_key, preferred_element_type=jnp.float32).astype(jnp.bfloat16)
     own_values = jnp.dot(merged, w_value, preferred_element_type=jnp.float32).astype(jnp.bfloat16)
     carry = start_state
-    keys = lax.all_gather(own_keys, "ctx", axis=0, tiled=True)
-    values = lax.all_gather(own_values, "ctx", axis=0, tiled=True)
+    keys, values = jnp.split(
+        lax.all_gather(jnp.concatenate([own_keys, own_values], axis=1), "ctx", axis=0, tiled=True),
+        [own_keys.shape[1]],
+        axis=1,
+    )
     bias = lax.all_gather(key_bias, "ctx", axis=0, tiled=True)
     length = keys.shape[0]
     block = math.gcd(length, 1536)

time: 127 us -> 119 us (0.937)
  blocking collectives: 91.4 us -> 47.1 us
  waiting for transfers between devices: 4.09 us -> 23.8 us
  between operations: 0.88 us -> 14.3 us
  local copies, waits for them, and re-layouts: 6.33 us -> 9.3 us
    all_gather x2 -> x0, blocking collectives: 41.9 us -> none  [the longest x1 21.5 us: on_device(): keys = lax.all_gather(own_keys, 'ctx', axis=0, tiled=True)]
    all_to_all x1, waiting for transfers between devices: 0.01 us -> 15 us  [on_device(): lax.all_to_all(outgoing.reshape(shards, slots, -1), 'ctx', split_axis=0,...]
    all_gather x0 -> x1, waiting for transfers between devices: none -> 4.67 us  [on_device(): lax.all_gather(jnp.concatenate([own_keys, own_values], axis=1), 'ctx', ax...]
    split x0 -> x3, local copies, waits for them, and re-layouts: none -> 4.56 us  [on_device(): jnp.split(lax.all_gather(jnp.concatenate([own_keys, own_values], axis=1),...]
    unnamed x1, blocking collectives: 35.8 us -> 32.6 us
    all_gather x2 -> x0, local copies, waits for them, and re-layouts: 1.88 us -> none  [the longest x1 1.29 us: on_device(): values = lax.all_gather(own_values, 'ctx', axis=0, tiled=True)]
    dot_general x1, matrix products: 1.8 us -> 0.47 us  [on_device(): jnp.dot(merged, w_query, preferred_element_type=jnp.float32)]
    dot_general x1, matrix products: 1.79 us -> 0.47 us  [on_device(): jnp.dot(merged, w_key, preferred_element_type=jnp.float32)]
  transfers between devices with their start and end apart: 2 -> 3, of which waited for: 1 -> 3; matrix products, arithmetic and copies ran while one was open for 3% -> 4% of each run, Pallas kernels for 0% -> 0%
where the time goes in v1:
time: 119 us
  blocking collectives  47.1 us (40%)
  waiting for transfers between devices  23.8 us (20%)
  between operations  14.3 us (12%)
  starting transfers between devices  11 us (9%)
  matrix products  9.66 us (8%)
  local copies, waits for them, and re-layouts  9.3 us (8%)
  other arithmetic  3.73 us (3%)
    unnamed x1, blocking collectives  32.6 us
    all_to_all x1, waiting for transfers between devices, on_device(): lax.all_to_all(outgoing.reshape(shards, slots, -1), 'ctx', split_axis=0,...  15 us
    all_to_all x1, blocking collectives, on_device(): lax.all_to_all(leaving.reshape(shards, slots, -1), 'ctx', split_axis=0, c...  14.5 us
    all_to_all x1, starting transfers between devices, on_device(): lax.all_to_all(out_weights.reshape(shards, slots), 'ctx', split_axis=0, c...  7.41 us
    all_gather x1, waiting for transfers between devices, on_device(): lax.all_gather(jnp.concatenate([own_keys, own_values], axis=1), 'ctx', ax...  4.67 us
    split x3, local copies, waits for them, and re-layouts, on_device(): jnp.split(lax.all_gather(jnp.concatenate([own_keys, own_values], axis=1),...  4.56 us
    all_to_all x1, waiting for transfers between devices, on_device(): lax.all_to_all(out_weights.reshape(shards, slots), 'ctx', split_axis=0, c...  4.1 us
    all_to_all x1, starting transfers between devices, on_device(): lax.all_to_all(outgoing.reshape(shards, slots, -1), 'ctx', split_axis=0,...  3.58 us
  transfers between devices with their start and end apart: 3, of which 3 were waited for; matrix products, arithmetic and copies ran while one was open for 4% of the time, Pallas kernels for 0%

profile of v1, /device:TPU:0, one launch (start us, length us, event | category | flops | bytes accessed | tf_op | source)
XLA Modules:
  0.0 118.9 jit_solution(1695023652842360894)
XLA Ops:
  6.5 0.0 copy-start
  6.5 0.8 fusion.16
  7.4 0.1 reduce_window_sum.11
  7.5 0.8 select_reduce_fusion
  8.4 0.7 fusion.23
  9.0 0.8 fusion.10
  9.9 0.7 all_to_all.16
  10.6 7.4 %all-to-all-start = ((bf16[16,1,12]{2,1,0:T(2,128)(2,1)}), bf16[16,1,12]{2,1,0:T(2,128)(2,1)S(1)}, u32[]{:S(2)}, u32[]{:S(2)}) async-start(bf16[16,1,12]{2,1,0:T(2,128)(2,1)} %all_to_all.16), calls=%async_computation | async-start | bytes 16384 | tf_op jit(solution)/shard_map/all_to_all | solution.py:34
  18.0 0.0 copy-start.4
  18.0 1.3 %convolution_convert_fusion = bf16[192,1152]{1,0:T(8,128)(2,1)S(1)} fusion(bf16[96,1152]{1,0:T(8,128)(2,1)} %param.8, s32[96]{0:T(128)S(1)} %fusion.23), kind=kOutput, calls=%fused_computation | convolution fusion | flops 42706944 | bytes 663936 | tf_op jit(solution)/shard_map/tp,td->pd/dot_general | solution.py:24
  19.4 0.9 reshape.49
  20.3 4.1 %all-to-all-done = bf16[16,1,12]{2,1,0:T(2,128)(2,1)S(1)} async-done(((bf16[16,1,12]{2,1,0:T(2,128)(2,1)}), bf16[16,1,12]{2,1,0:T(2,128)(2,1)S(1)}, u32[]{:S(2)}, u32[]{:S(2)}) %all-to-all-start) | async-done | bytes 416 | tf_op jit(solution)/shard_map/all_to_all | solution.py:34
  24.4 3.6 %all-to-all-start.1 = ((bf16[16,12,1152]{2,1,0:T(8,128)(2,1)}), bf16[16,12,1152]{2,1,0:T(8,128)(2,1)S(1)}, u32[]{:S(2)}, u32[]{:S(2)}) async-start(bf16[16,12,1152]{2,1,0:T(8,128)(2,1)} %reshape.49), calls=%async_computation.1 | async-start | bytes 1179648 | tf_op jit(solution)/shard_map/all_to_all | solution.py:31
  28.0 0.0 copy-start.1
  28.0 0.0 all-gather.2.cloned.1.call-start
  28.0 0.0 copy-done.4
  28.0 0.1 copy.23
  28.1 0.1 eq.53
  28.2 0.1 broadcast_in_dim.39
  28.3 0.1 convert_reduce_fusion
  28.5 15.0 %all-to-all-done.1 = bf16[16,12,1152]{2,1,0:T(8,128)(2,1)S(1)} async-done(((bf16[16,12,1152]{2,1,0:T(8,128)(2,1)}), bf16[16,12,1152]{2,1,0:T(8,128)(2,1)S(1)}, u32[]{:S(2)}, u32[]{:S(2)}) %all-to-all-start.1) | async-done | bytes 442400 | tf_op jit(solution)/shard_map/all_to_all | solution.py:31
  43.4 0.9 reshape.50
  44.3 0.0 copy-start.2
  44.3 1.3 %fusion = bf16[48,1152]{1,0:T(8,128)(2,1)S(1)} fusion(bf16[192,1152]{1,0:T(8,128)(2,1)} %reshape.50, f32[48]{0:T(128)S(1)} %get-tuple-element.22, s32[192]{0:T(256)S(1)} %eq.53, bf16[192]{0:T(256)(128)(2,1)S(1)} %broadcast_in_dim.39), kind=kOutput, calls=%fused_computation.3 | convolution fusion | flops 21362688 | bytes 554304 | tf_op jit(solution)/shard_map/dot_general | solution.py:41
  45.6 0.0 copy-done.1
  45.6 0.0 copy-start.5
  45.7 0.5 convolution_convert_fusion.4
  46.1 0.0 copy-done.2
  46.1 0.0 copy-start.3
  46.2 0.5 convolution_convert_fusion.5
  46.6 0.7 pad_maximum_fusion
  47.4 0.0 all-gather.2.cloned.1.call-update
  47.4 0.0 copy-done.5
  47.4 0.6 dynamic-slice.1
  48.7 0.2 dynamic-update-slice
  48.9 32.6 %all-reduce = bf16[768]{0:T(1024)(128)(2,1)S(1)} all-reduce(bf16[768]{0:T(1024)(128)(2,1)S(1)} %dynamic-update-slice), channel_id=1, replica_groups=mesh['groups'=2,'ctx'=16] {'ctx'}, use_global_device_ids=true, to_apply=%add | all-reduce | flops 768 | bytes 3072
  81.5 0.0 copy-done.3
  81.5 0.5 convolution_convert_fusion.6
  82.0 0.8 reshape.51
  82.8 4.7 %all-gather.2.cloned.1.call-done = bf16[768,1152]{1,0:T(8,128)(2,1)} async-done(((bf16[48,1152]{1,0:T(8,128)(2,1)}), bf16[768,1152]{1,0:T(8,128)(2,1)}) %all-gather.2.cloned.1.call-update) | async-done | bytes 1769488 | tf_op jit(solution)/shard_map/all_gather | solution.py:78
  87.4 2.0 %fusion.25 = (bf16[768,576]{1,0:T(8,128)(2,1)S(1)}, bf16[768,576]{1,0:T(8,128)(2,1)S(1)}) fusion(bf16[768,1152]{1,0:T(8,128)(2,1)} %all-gather.2.cloned.1.call-done), kind=kLoop, calls=%fused_computation.45 | loop fusion | bytes 3538944 | tf_op jit(solution)/shard_map/split | solution.py:77
  89.4 1.3 %copy.25 = bf16[768,576]{0,1:T(8,128)(2,1)} copy(bf16[768,576]{1,0:T(8,128)(2,1)S(1)} %get-tuple-element.19) | data formatting | bytes 1769472 | tf_op jit(solution)/shard_map/split | solution.py:77
  90.7 1.6 %fusion.26 = (f32[8,48]{1,0:T(8,128)S(1)}, f32[8,48,768]{2,1,0:T(8,128)S(1)}) fusion(f32[768]{0:T(1024)S(1)} %convert_element_type.69, bf16[768,8,72]{0,2,1:T(8,128)(2,1)} %bitcast.41, bf16[48,8,72]{2,1,0:T(8,128)(2,1)} %reshape.51), kind=kOutput, calls=%fused_computation.46 | convolution fusion | flops 43351680 | bytes 2124288 | tf_op jit(solution)/shard_map/while/body/eval_jaxpr/qhd,khd->hqk/dot_general | solution.py:53
  92.3 0.3 fusion.5
  92.7 1.3 %copy.27 = bf16[768,576]{0,1:T(8,128)(2,1)} copy(bf16[768,576]{1,0:T(8,128)(2,1)S(1)} %get-tuple-element.20) | data formatting | bytes 1769472 | tf_op jit(solution)/shard_map/split | solution.py:77
  94.0 1.6 %fusion.4 = bf16[48,8,72]{2,0,1:T(8,128)(2,1)S(1)} fusion(bf16[768,8,72]{0,2,1:T(8,128)(2,1)} %bitcast.42, f32[8,48,768]{2,1,0:T(8,128)S(1)} %get-tuple-element.32, f32[8,48]{1,0:T(8,128)S(1)} %get-tuple-element.23, f32[48,8]{0,1:T(8,128)S(1)} %bitcast_add_fusion, f32[48,8]{0,1:T(8,128)S(1)} %multiply_bitcast_fusion), kind=kOutput, calls=%fused_computation.12 | convolution fusion | flops 43140096 | bytes 2124288 | tf_op jit(solution)/shard_map/while/body/eval_jaxpr/hqk,khd->hqd/dot_general | solution.py:61
  95.6 0.1 convert_element_type.72
  95.8 0.3 convolution_convert_fusion.2
  96.1 0.1 reshape.52
  96.1 14.5 %all_to_all.20 = bf16[16,12,576]{2,1,0:T(8,128)(2,1)S(1)} all-to-all(bf16[16,12,576]{2,1,0:T(8,128)(2,1)S(1)} %reshape.52), channel_id=1, replica_groups=mesh['groups'=2,'ctx'=16] {'ctx'}, dimensions={0} | all-to-all | bytes 442368 | tf_op jit(solution)/shard_map/all_to_all | solution.py:102
  110.7 0.1 reshape.53
  110.8 0.0 copy-done
  110.8 1.2 %convolution_convert_fusion.1 = bf16[96,1152]{1,0:T(8,128)(2,1)} fusion(bf16[576,1152]{1,0:T(8,128)(2,1)S(1)} %copy-done, bf16[192,576]{1,0:T(8,128)(2,1)S(1)} %reshape.53, s32[96]{0:T(128)S(1)} %fusion.23), kind=kOutput, calls=%fused_computation.1 | convolution fusion | flops 148819968 | bytes 1769856 | tf_op jit(solution)/shard_map/dot_general | solution.py:108
  (8 shorter events, 0.1 us)
Async XLA Ops:
  6.5 104.2 %copy-start = (bf16[576,1152]{1,0:T(8,128)(2,1)S(1)}, bf16[576,1152]{1,0:T(8,128)(2,1)}, u32[]{:S(2)}) copy-start(bf16[576,1152]{1,0:T(8,128)(2,1)} %param.15) | copy-start | bytes 3981316
  10.6 13.8 %all-to-all-start = ((bf16[16,1,12]{2,1,0:T(2,128)(2,1)}), bf16[16,1,12]{2,1,0:T(2,128)(2,1)S(1)}, u32[]{:S(2)}, u32[]{:S(2)}) async-start(bf16[16,1,12]{2,1,0:T(2,128)(2,1)} %all_to_all.16), calls=%async_computation | async-start | bytes 16384 | tf_op jit(solution)/shard_map/all_to_all | solution.py:34
  18.0 10.0 %copy-start.4 = (s32[1,16,12]{1,0,2:T(1,128)S(1)}, s32[1,16,12]{1,0,2:T(1,128)}, u32[]{:S(2)}) copy-start(s32[1,16,12]{1,0,2:T(1,128)} %param.10) | copy-start | bytes 2308
  24.4 19.1 %all-to-all-start.1 = ((bf16[16,12,1152]{2,1,0:T(8,128)(2,1)}), bf16[16,12,1152]{2,1,0:T(8,128)(2,1)S(1)}, u32[]{:S(2)}, u32[]{:S(2)}) async-start(bf16[16,12,1152]{2,1,0:T(8,128)(2,1)} %reshape.49), calls=%async_computation.1 | async-start | bytes 1179648 | tf_op jit(solution)/shard_map/all_to_all | solution.py:31
  28.0 17.7 %copy-start.1 = (bf16[1152,576]{0,1:T(8,128)(2,1)S(1)}, bf16[1152,576]{0,1:T(8,128)(2,1)}, u32[]{:S(2)}) copy-start(bf16[1152,576]{0,1:T(8,128)(2,1)} %param.14) | copy-start | bytes 3981316
  28.0 59.5 %all-gather.2.cloned.1.call-start = ((), (), s32[]{:S(2)}) async-start(), calls=%async_computation.3 | async-start | bytes 1880064 | tf_op jit(solution)/shard_map/all_gather | solution.py:78
  44.3 1.8 %copy-start.2 = (bf16[1152,576]{0,1:T(8,128)(2,1)S(1)}, bf16[1152,576]{0,1:T(8,128)(2,1)}, u32[]{:S(2)}) copy-start(bf16[1152,576]{0,1:T(8,128)(2,1)} %param.13) | copy-start | bytes 3981316
  45.6 1.8 %copy-start.5 = (u32[32]{0:T(128)S(1)}, u32[32]{0:T(128)}, u32[]{:S(2)}) copy-start(u32[32]{0:T(128)} %constant.40) | copy-start | bytes 388
  46.1 35.4 %copy-start.3 = (bf16[1152,576]{0,1:T(8,128)(2,1)S(1)}, bf16[1152,576]{0,1:T(8,128)(2,1)}, u32[]{:S(2)}) copy-start(bf16[1152,576]{0,1:T(8,128)(2,1)} %param.12) | copy-start | bytes 3981316
Sparse Core Ops, SparseCore 0:
  47.5 39.8 all-gather.1
